TPU v7x, 128 devices: a whole 4x4x4 slice. The times are simulated.
128 devices in a mesh: fsdp: 64 (over z, x_hi, y, core), tensor: 2 (over x_lo).
Axes of the slice: x: 4 (x_hi: 2, x_lo: 2; x = x_hi * 2 + x_lo), y: 4, z: 4, core: 2. Of those that a mesh axis runs over, the one named last changes fastest.
Arguments:
- tokens: bfloat16 [8192, 1024], P('fsdp'), may hold values from -6 to 6
- segment: int32 [8192], P('fsdp'), may hold values from 0 to 8191, as said below
- w_query: bfloat16 [1024, 1024], P('fsdp', 'tensor'), may hold values from -0.1875 to 0.1875
- w_key: bfloat16 [1024, 512], P('fsdp', 'tensor'), may hold values from -0.1875 to 0.1875
- w_value: bfloat16 [1024, 512], P('fsdp', 'tensor'), may hold values from -0.1875 to 0.1875
- w_output: bfloat16 [1024, 1024], P('tensor', 'fsdp'), may hold values from -0.5 to 0.5
- w_gate: bfloat16 [1024, 4608], P('fsdp', 'tensor'), may hold values from -0.1875 to 0.1875
- w_up: bfloat16 [1024, 4608], P('fsdp', 'tensor'), may hold values from -0.1875 to 0.1875
- w_down: bfloat16 [4608, 1024], P('tensor', 'fsdp'), may hold values from -0.09375 to 0.09375
- norm_attn: bfloat16 [1024], P('fsdp'), may hold values from 0.25 to 1.75
- norm_ffn: bfloat16 [1024], P('fsdp'), may hold values from 0.25 to 1.75
- norm_query: bfloat16 [64], P('fsdp'), may hold values from 0.25 to 1.75
- norm_key: bfloat16 [64], P('fsdp'), may hold values from 0.25 to 1.75
- cotangent: bfloat16 [8192, 1024], P('fsdp'), may hold values from -16 to 16
Outputs:
- block_out: bfloat16 [8192, 1024], P('fsdp')
- grad_tokens: bfloat16 [8192, 1024], P('fsdp')
- grad_query: float32 [1024, 1024], P('fsdp', 'tensor')
- grad_key: float32 [1024, 512], P('fsdp', 'tensor')
- grad_value: float32 [1024, 512], P('fsdp', 'tensor')
- grad_output: float32 [1024, 1024], P('tensor', 'fsdp')
- grad_gate: float32 [1024, 4608], P('fsdp', 'tensor')
- grad_up: float32 [1024, 4608], P('fsdp', 'tensor')
- grad_down: float32 [4608, 1024], P('tensor', 'fsdp')
- grad_norm_attn: float32 [1024], P('fsdp')
- grad_norm_ffn: float32 [1024], P('fsdp')
- grad_norm_query: float32 [64], P('fsdp')
- grad_norm_key: float32 [64], P('fsdp')
Inputs may be any that keep to these rules, and one draw needn't show every extreme that they name: `segment`: ids never fall; all tokens of an id lie in one aligned block of 128 tokens; the first and the last token of every such block start a new id.
All inputs are finite; a program needn't handle non-finite values.
Results may differ from a plain program's by a relative error of at most 0.019.
Values may be sent and summed in bfloat16 or wider, within the bound.
No kernel may reach another device: no remote copies, remote signals or barrier semaphores. Data moves between devices by JAX's collectives and lax.ppermute only.
A program may use at most 128 MiB of HBM per device.

v0:
```python
import jax
import jax.numpy as jnp
from jax import lax
from jax.sharding import PartitionSpec as P

epsilon = 1e-05
rope_base = 1000000.0


def matmul(matrix, second):
    return jnp.dot(matrix, second, preferred_element_type=jnp.float32)


def matmul_tr(matrix, second):
    return lax.dot_general(
        matrix, second, (((1,), (1,)), ((), ())), preferred_element_type=jnp.float32
    )


def tr_matmul(matrix, second):
    return lax.dot_general(
        matrix, second, (((0,), (0,)), ((), ())), preferred_element_type=jnp.float32
    )


def contract(pattern, matrix, second):
    return jnp.einsum(pattern, matrix, second, preferred_element_type=jnp.float32)


def normalize(vector):
    inverse = lax.rsqrt(jnp.mean(vector * vector, axis=-1, keepdims=True) + epsilon)
    return (vector * inverse, inverse)


def norm_back(grad_in, normed, inverse):
    return inverse * (grad_in - normed * jnp.mean(grad_in * normed, axis=-1, keepdims=True))


def rotate(vector):
    half_size = vector.shape[-1] // 2
    return jnp.concatenate([-vector[..., half_size:], vector[..., :half_size]], axis=-1)


def rotate_back(vector):
    half_size = vector.shape[-1] // 2
    return jnp.concatenate([vector[..., half_size:], -vector[..., :half_size]], axis=-1)


def tables(segment, head_size):
    row_count = segment.shape[0]
    row_index = jnp.arange(row_count, dtype=jnp.int32)
    same_segment = segment[:, None] == segment[None, :]
    first_row = jnp.min(jnp.where(same_segment, row_index[None, :], row_count), axis=1)
    position = (row_index - first_row).astype(jnp.float32)
    allowed = same_segment & (row_index[None, :] <= row_index[:, None])
    half_size = head_size // 2
    frequency = jnp.power(rope_base, -2.0 * jnp.arange(half_size, dtype=jnp.float32) / head_size)
    phase_angle = position[:, None] * frequency[None, :]
    phase_angle = jnp.concatenate([phase_angle, phase_angle], axis=1)
    return (allowed, jnp.cos(phase_angle)[:, None, :], jnp.sin(phase_angle)[:, None, :])


def head_prep(raw_heads, head_gain, cos_table, sin_table):
    unit_heads, inverse = normalize(raw_heads)
    scaled = unit_heads * head_gain
    return (scaled * cos_table + rotate(scaled) * sin_table, unit_heads, inverse)


def head_back(grad_in, unit_heads, inverse, head_gain, cos_table, sin_table):
    grad_scaled = grad_in * cos_table + rotate_back(grad_in * sin_table)
    gain_grad = jnp.sum(grad_scaled * unit_heads, axis=(0, 1))
    return (norm_back(grad_scaled * head_gain, unit_heads, inverse), gain_grad)


def score_block(query_heads, key_heads, allowed):
    row_count, head_count, head_size = query_heads.shape
    kv_count = key_heads.shape[1]
    query_groups = query_heads.reshape(row_count, kv_count, head_count // kv_count, head_size)
    scores = contract("ikgd,jkd->kgij", query_groups, key_heads) * head_size ** (-0.5)
    return (query_groups, jnp.where(allowed, scores, -1e30))


def attend(query_heads, key_heads, value_heads, allowed):
    row_count, head_count, head_size = query_heads.shape
    query_groups, masked = score_block(query_heads, key_heads, allowed)
    row_max = jnp.max(masked, axis=-1, keepdims=True)
    exp_scores = jnp.exp(masked - row_max)
    denominator = jnp.sum(exp_scores, axis=-1, keepdims=True)
    log_total = row_max + jnp.log(denominator)
    attn_weights = (exp_scores / denominator).astype(jnp.bfloat16)
    mixed = contract("kgij,jkd->ikgd", attn_weights, value_heads).astype(jnp.bfloat16)
    return (mixed.reshape(row_count, head_count * head_size), log_total)


def attend_back(query_heads, key_heads, value_heads, attended, grad_attended, log_total, allowed):
    row_count, head_count, head_size = query_heads.shape
    kv_count = key_heads.shape[1]
    group_size = head_count // kv_count
    query_groups, masked = score_block(query_heads, key_heads, allowed)
    prob = jnp.exp(masked - log_total)
    prob_low = prob.astype(jnp.bfloat16)
    grad_groups = grad_attended.reshape(row_count, kv_count, group_size, head_size)
    out_groups = attended.reshape(row_count, kv_count, group_size, head_size)
    row_delta = jnp.sum(grad_groups.astype(jnp.float32) * out_groups.astype(jnp.float32), axis=-1)
    row_delta = jnp.transpose(row_delta, (1, 2, 0))[..., None]
    grad_kv_value = contract("kgij,ikgd->jkd", prob_low, grad_groups)
    grad_prob = contract("ikgd,jkd->kgij", grad_groups, value_heads)
    grad_scores = (prob * (grad_prob - row_delta) * head_size ** (-0.5)).astype(jnp.bfloat16)
    grad_query = contract("kgij,jkd->ikgd", grad_scores, key_heads).reshape(
        row_count, head_count, head_size
    )
    grad_key = contract("kgij,ikgd->jkd", grad_scores, query_groups)
    return (grad_query, grad_key, grad_kv_value)


def on_device(
    tokens,
    segment,
    w_query,
    w_key,
    w_value,
    w_output,
    w_gate,
    w_up,
    w_down,
    norm_attn,
    norm_ffn,
    norm_query,
    norm_key,
    cotangent,
):
    shards = (
        w_query,
        w_key,
        w_value,
        w_gate,
        w_up,
        w_output,
        w_down,
        norm_attn,
        norm_ffn,
        norm_query,
        norm_key,
    )
    gathered = (
        lax.all_gather(shards[0], "fsdp", axis=0, tiled=True),
        lax.all_gather(shards[1], "fsdp", axis=0, tiled=True),
        lax.all_gather(shards[2], "fsdp", axis=0, tiled=True),
        lax.all_gather(shards[3], "fsdp", axis=0, tiled=True),
        lax.all_gather(shards[4], "fsdp", axis=0, tiled=True),
        lax.all_gather(shards[5], "fsdp", axis=1, tiled=True),
        lax.all_gather(shards[6], "fsdp", axis=1, tiled=True),
        lax.all_gather(shards[7], "fsdp", axis=0, tiled=True),
        lax.all_gather(shards[8], "fsdp", axis=0, tiled=True),
        lax.all_gather(shards[9], "fsdp", axis=0, tiled=True),
        lax.all_gather(shards[10], "fsdp", axis=0, tiled=True),
    )
    (
        full_query,
        full_key,
        full_value,
        full_gate,
        full_up,
        full_output,
        full_down,
        gain_attn,
        gain_ffn,
        gain_query,
        gain_key,
    ) = gathered
    row_count = tokens.shape[0]
    head_size = gain_query.shape[0]
    head_count = full_query.shape[1] // head_size
    kv_count = full_key.shape[1] // head_size
    allowed, cos_table, sin_table = tables(segment, head_size)
    inputs = tokens.astype(jnp.float32)
    normed_one, inv_one = normalize(inputs)
    hidden_one = (normed_one * gain_attn).astype(jnp.bfloat16)
    query_raw = matmul(hidden_one, full_query).reshape(row_count, head_count, head_size)
    key_raw = matmul(hidden_one, full_key).reshape(row_count, kv_count, head_size)
    value_heads = (
        matmul(hidden_one, full_value).astype(jnp.bfloat16).reshape(row_count, kv_count, head_size)
    )
    query_rot, query_unit, query_inv = head_prep(query_raw, gain_query, cos_table, sin_table)
    key_rot, key_unit, key_inv = head_prep(key_raw, gain_key, cos_table, sin_table)
    query_heads = query_rot.astype(jnp.bfloat16)
    key_heads = key_rot.astype(jnp.bfloat16)
    attended, log_total = attend(query_heads, key_heads, value_heads, allowed)
    residual = inputs + lax.psum(matmul(attended, full_output), "tensor")
    normed_two, inv_two = normalize(residual)
    hidden_two = (normed_two * gain_ffn).astype(jnp.bfloat16)
    gate_pre = matmul(hidden_two, full_gate)
    up_pre = matmul(hidden_two, full_up)
    sigmoid_gate = jax.nn.sigmoid(gate_pre)
    activation = (gate_pre * sigmoid_gate * up_pre).astype(jnp.bfloat16)
    ffn_result = lax.psum(matmul(activation, full_down).astype(jnp.bfloat16), "tensor").astype(
        jnp.float32
    )
    block_out = (residual + ffn_result).astype(jnp.bfloat16)
    (
        back_query,
        back_key,
        back_value,
        back_gate,
        back_up,
        back_output,
        back_down,
        back_attn,
        back_ffn,
        back_qgain,
        back_kgain,
    ) = gathered
    grad_act = matmul_tr(cotangent, back_down)
    grad_gate_pre = (
        grad_act * up_pre * sigmoid_gate * (1.0 + gate_pre * (1.0 - sigmoid_gate))
    ).astype(jnp.bfloat16)
    grad_up_pre = (grad_act * gate_pre * sigmoid_gate).astype(jnp.bfloat16)
    partial_two = matmul_tr(grad_gate_pre, back_gate) + matmul_tr(grad_up_pre, back_up)
    grad_hidden_two = lax.psum(partial_two, "tensor")
    grad_norm_ffn = jnp.sum(grad_hidden_two * normed_two, axis=0)
    ffn_width = grad_gate_pre.shape[1]
    grad_residual = cotangent.astype(jnp.float32) + norm_back(
        grad_hidden_two * back_ffn, normed_two, inv_two
    )
    grad_res_low = grad_residual.astype(jnp.bfloat16)
    grad_attended = matmul_tr(grad_res_low, back_output).astype(jnp.bfloat16)
    grad_q_rot, grad_k_rot, grad_kv_value = attend_back(
        query_heads, key_heads, value_heads, attended, grad_attended, log_total, allowed
    )
    grad_q_raw, part_norm_query = head_back(
        grad_q_rot, query_unit, query_inv, back_qgain, cos_table, sin_table
    )
    grad_k_raw, part_norm_key = head_back(
        grad_k_rot, key_unit, key_inv, back_kgain, cos_table, sin_table
    )
    query_low = grad_q_raw.reshape(row_count, head_count * head_size).astype(jnp.bfloat16)
    key_low = grad_k_raw.reshape(row_count, kv_count * head_size).astype(jnp.bfloat16)
    value_low = grad_kv_value.reshape(row_count, kv_count * head_size).astype(jnp.bfloat16)
    partial_one = (
        matmul_tr(query_low, back_query)
        + matmul_tr(key_low, back_key)
        + matmul_tr(value_low, back_value)
    )
    grad_hidden_one, grad_norm_query, grad_norm_key = lax.psum(
        (partial_one, part_norm_query, part_norm_key), "tensor"
    )
    grad_norm_attn = jnp.sum(grad_hidden_one * normed_one, axis=0)
    grad_tokens = (
        grad_residual + norm_back(grad_hidden_one * back_attn, normed_one, inv_one)
    ).astype(jnp.bfloat16)
    query_width = query_low.shape[1]
    key_width = key_low.shape[1]
    whole_owned = lax.psum_scatter(
        jnp.concatenate(
            [
                jnp.concatenate(
                    [
                        tr_matmul(hidden_one, query_low),
                        tr_matmul(hidden_one, key_low),
                        tr_matmul(hidden_one, value_low),
                        tr_matmul(grad_res_low, attended),
                    ],
                    axis=1,
                ),
                jnp.concatenate(
                    [
                        tr_matmul(hidden_two, grad_gate_pre),
                        tr_matmul(hidden_two, grad_up_pre),
                        tr_matmul(cotangent, activation),
                    ],
                    axis=1,
                ),
            ],
            axis=1,
        ),
        "fsdp",
        scatter_dimension=0,
        tiled=True,
    )
    attn_width = 2 * query_width + 2 * key_width
    attn_owned = whole_owned[:, :attn_width]
    ffn_owned = whole_owned[:, attn_width:]
    gain_owned = (
        lax.psum_scatter(grad_norm_attn, "fsdp", scatter_dimension=0, tiled=True),
        lax.psum_scatter(grad_norm_ffn, "fsdp", scatter_dimension=0, tiled=True),
        lax.psum_scatter(grad_norm_query, "fsdp", scatter_dimension=0, tiled=True),
        lax.psum_scatter(grad_norm_key, "fsdp", scatter_dimension=0, tiled=True),
    )
    grad_query = attn_owned[:, :query_width]
    grad_key = attn_owned[:, query_width : query_width + key_width]
    grad_value = attn_owned[:, query_width + key_width : query_width + 2 * key_width]
    grad_output = attn_owned[:, query_width + 2 * key_width :].T
    grad_gate = ffn_owned[:, :ffn_width]
    grad_up = ffn_owned[:, ffn_width : 2 * ffn_width]
    grad_down = ffn_owned[:, 2 * ffn_width :].T
    return (
        block_out,
        grad_tokens,
        grad_query,
        grad_key,
        grad_value,
        grad_output,
        grad_gate,
        grad_up,
        grad_down,
        gain_owned[0],
        gain_owned[1],
        gain_owned[2],
        gain_owned[3],
    )


def solution(mesh):
    return jax.shard_map(
        on_device,
        mesh=mesh,
        in_specs=(
            P("fsdp", None),
            P("fsdp"),
            P("fsdp", "tensor"),
            P("fsdp", "tensor"),
            P("fsdp", "tensor"),
            P("tensor", "fsdp"),
            P("fsdp", "tensor"),
            P("fsdp", "tensor"),
            P("tensor", "fsdp"),
            P("fsdp"),
            P("fsdp"),
            P("fsdp"),
            P("fsdp"),
            P("fsdp", None),
        ),
        out_specs=(
            P("fsdp", None),
            P("fsdp", None),
            P("fsdp", "tensor"),
            P("fsdp", "tensor"),
            P("fsdp", "tensor"),
            P("tensor", "fsdp"),
            P("fsdp", "tensor"),
            P("fsdp", "tensor"),
            P("tensor", "fsdp"),
            P("fsdp"),
            P("fsdp"),
            P("fsdp"),
            P("fsdp"),
        ),
        check_vma=False,
    )
```

profile of v0, /device:TPU:0, one launch (start us, length us, event | category | flops | bytes accessed | tf_op | source)
XLA Modules:
  0.0 1088.6 jit_solution(5932731994119234216)
XLA Ops:
  17.2 173.2 %all-reduce.10 = (bf16[1024]{0:T(1024)(128)(2,1)S(1)}, bf16[64]{0:T(256)(128)(2,1)S(1)}, bf16[64]{0:T(256)(128)(2,1)S(1)}, bf16[1024]{0:T(1024)(128)(2,1)S(1)}) all-reduce(bf16[1024]{0:T(1024)(128)(2,1)S(1)} %dynamic-update-slice, bf16[64]{0:T(256)(128)(2,1)S(1)} %dynamic-update-slice.1, ...), channel_id=1, replica_groups=mesh['fsdp'=64,'tensor'=2] {'fsdp'}, use_global_device_ids=true, to_apply=%add | all-reduce | flops 2176 | bytes 8704
  190.6 89.9 %all_gather.35 = bf16[1024,256]{1,0:T(8,128)(2,1)S(1)} all-gather(bf16[16,256]{1,0:T(8,128)(2,1)} %param.17), channel_id=1, replica_groups=mesh['fsdp'=64,'tensor'=2] {'fsdp'}, dimensions={0}, use_global_device_ids=true | all-gather | bytes 532480 | tf_op jit(solution)/shard_map/all_gather | solution.py:147
  282.0 91.7 %all_gather.34 = bf16[1024,256]{1,0:T(8,128)(2,1)S(1)} all-gather(bf16[16,256]{1,0:T(8,128)(2,1)} %param.18), channel_id=1, replica_groups=mesh['fsdp'=64,'tensor'=2] {'fsdp'}, dimensions={0}, use_global_device_ids=true | all-gather | bytes 532480 | tf_op jit(solution)/shard_map/all_gather | solution.py:148
  379.6 2.5 fusion.47
  386.3 25.0 %all-reduce.16.cloned.1.call-done = f32[128,1024]{1,0:T(8,128)} async-done(((f32[128,1024]{1,0:T(8,128)}), f32[128,1024]{1,0:T(8,128)}) %all-reduce.16.cloned.1.call-update) | async-done | bytes 524304 | tf_op jit(solution)/shard_map/psum | solution.py:189
  413.2 75.6 %all-gather.12.cloned.1.call-done = bf16[1024,2304]{1,0:T(8,128)(2,1)} async-done(((bf16[16,2304]{1,0:T(8,128)(2,1)}), bf16[1024,2304]{1,0:T(8,128)(2,1)}) %all-gather.12.cloned.1.call-update) | async-done | bytes 4718608 | tf_op jit(solution)/shard_map/all_gather | solution.py:150
  488.8 4.2 fusion.49
  492.9 70.8 %all-gather.10.cloned.1.call-done = bf16[1024,2304]{1,0:T(8,128)(2,1)} async-done(((bf16[16,2304]{1,0:T(8,128)(2,1)}), bf16[1024,2304]{1,0:T(8,128)(2,1)}) %all-gather.10.cloned.1.call-update) | async-done | bytes 4718608 | tf_op jit(solution)/shard_map/all_gather | solution.py:149
  563.7 4.1 fusion.48
  567.9 70.8 %all-gather.14.cloned.1.call-done = bf16[2304,1024]{0,1:T(8,128)(2,1)} async-done(((bf16[2304,16]{0,1:T(8,128)(2,1)}), bf16[2304,1024]{0,1:T(8,128)(2,1)}) %all-gather.14.cloned.1.call-update) | async-done | bytes 4718608 | tf_op jit(solution)/shard_map/all_gather | solution.py:152
  638.7 5.1 multiply_convert_fusion
  645.5 4.8 convolution_add_fusion.1
  651.6 4.9 convolution_convert_fusion
  656.8 27.3 %all-reduce.20.cloned.1.call-done = f32[128,1024]{1,0:T(8,128)} async-done(((f32[128,1024]{1,0:T(8,128)}), f32[128,1024]{1,0:T(8,128)}) %all-reduce.20.cloned.1.call-update) | async-done | bytes 524304 | tf_op jit(solution)/shard_map/psum | solution.py:219
  686.5 31.4 %all-reduce.18.cloned.1.call-done = bf16[128,1024]{1,0:T(8,128)(2,1)} async-done(((bf16[128,1024]{1,0:T(8,128)(2,1)}), bf16[128,1024]{1,0:T(8,128)(2,1)}) %all-reduce.18.cloned.1.call-update) | async-done | bytes 262160 | tf_op jit(solution)/shard_map/psum | solution.py:196
  736.8 2.5 fusion
  740.8 2.3 convolution_dynamic-update-slice_fusion.4
  745.0 5.1 convolution_dynamic-update-slice_fusion.1
  750.1 5.0 convolution_dynamic-update-slice_fusion
  755.2 5.1 bitcast_dynamic-update-slice_fusion
  760.3 15.3 %all-reduce.22.cloned.1.call-done = f32[128,1024]{1,0:T(8,128)} async-done(((f32[128,1024]{1,0:T(8,128)}), f32[128,1024]{1,0:T(8,128)}) %all-reduce.22.cloned.1.call-update) | async-done | bytes 524304 | tf_op jit(solution)/shard_map/psum | solution.py:244
  777.0 174.7 %all-reduce.8 = (f32[1024]{0:T(1024)S(1)}, f32[1024]{0:T(1024)S(1)}, f32[64]{0:T(128)S(1)}, f32[64]{0:T(128)S(1)}) all-reduce(f32[1024]{0:T(1024)S(1)} %get-tuple-element.15, f32[1024]{0:T(1024)S(1)} %copy-done.19, f32[64]{0:T(128)S(1)} %get-tuple-element.17, f32[64]{0:T(128)S(1)} %copy-done.25), channel_id=3, replica_groups=mesh['fsdp'=64,'tensor'=2] {'fsdp'}, use_global_device_ids=true, to_apply=%region_18.19.clone | all-reduce | flops 2176 | bytes 17408
  954.8 5.6 all-reduce.9
  963.6 113.6 %reduce-scatter.2.cloned.1.call-done = f32[16,8448]{1,0:T(8,128)} async-done(((f32[1024,8448]{1,0:T(8,128)}), f32[16,8448]{1,0:T(8,128)}) %reduce-scatter.2.cloned.1.call-update) | async-done | bytes 540688 | tf_op jit(solution)/shard_map/reduce_scatter | solution.py:253
  (162 shorter events, 60.6 us)
Async XLA Ops:
  7.2 369.6 %all-gather.6.cloned.1.call-start = ((), (), s32[]{:S(2)}) async-start(), calls=%async_computation.1 | async-start | bytes 1064960 | tf_op jit(solution)/shard_map/all_gather | solution.py:146
  7.9 371.7 %all-gather.8.cloned.1.call-start = ((), (), s32[]{:S(2)}) async-start(), calls=%async_computation.2 | async-start | bytes 1064960 | tf_op jit(solution)/shard_map/all_gather | solution.py:151
  8.7 402.7 %all-reduce.16.cloned.1.call-start = ((), (), s32[]{:S(2)}) async-start(), calls=%async_computation.3 | async-start | bytes 1048576 | tf_op jit(solution)/shard_map/psum | solution.py:189
  12.0 366.6 %copy-start.16 = (f32[128]{0:T(128)}, f32[128]{0:T(128)S(1)}, u32[]{:S(2)}) copy-start(f32[128]{0:T(128)S(1)} %add_rsqrt_fusion.3) | copy-start | bytes 1540
  190.4 188.4 %copy-start.20 = (f32[64]{0:T(128)}, f32[64]{0:T(128)S(1)}, u32[]{:S(2)}) copy-start(f32[64]{0:T(128)S(1)} %convert_element_type.115) | copy-start | bytes 772
  190.4 188.9 %copy-start.21 = (f32[64]{0:T(128)}, f32[64]{0:T(128)S(1)}, u32[]{:S(2)}) copy-start(f32[64]{0:T(128)S(1)} %convert_element_type.118) | copy-start | bytes 772
  375.8 6.3 copy-start.14
  378.6 32.7 %copy-start = (bf16[128,1024]{1,0:T(8,128)(2,1)S(1)}, bf16[128,1024]{1,0:T(8,128)(2,1)}, u32[]{:S(2)}) copy-start(bf16[128,1024]{1,0:T(8,128)(2,1)} %param.14) | copy-start | bytes 786436
  379.6 33.0 %copy-start.9 = (bf16[4,64,2,128]{3,1,2,0:T(8,128)(2,1)}, bf16[4,64,2,128]{3,1,2,0:T(8,128)(2,1)S(1)}, u32[]{:S(2)}) copy-start(bf16[4,64,2,128]{3,1,2,0:T(8,128)(2,1)S(1)} %convolution_convert_fusion.2) | copy-start | bytes 393220
  382.2 106.6 %all-gather.12.cloned.1.call-start = ((), (), s32[]{:S(2)}) async-start(), calls=%async_computation.5 | async-start | bytes 4792320 | tf_op jit(solution)/shard_map/all_gather | solution.py:150
  382.8 181.0 %all-gather.10.cloned.1.call-start = ((), (), s32[]{:S(2)}) async-start(), calls=%async_computation.4 | async-start | bytes 4792320 | tf_op jit(solution)/shard_map/all_gather | solution.py:149
  383.3 255.3 %all-gather.14.cloned.1.call-start = ((), (), s32[]{:S(2)}) async-start(), calls=%async_computation.6 | async-start | bytes 4792320 | tf_op jit(solution)/shard_map/all_gather | solution.py:152
  383.9 300.2 %all-reduce.20.cloned.1.call-start = ((), (), s32[]{:S(2)}) async-start(), calls=%async_computation.8 | async-start | bytes 1048576 | tf_op jit(solution)/shard_map/psum | solution.py:219
  413.2 225.5 %copy-start.11 = (bf16[128,1024]{1,0:T(8,128)(2,1)S(1)}, bf16[128,1024]{1,0:T(8,128)(2,1)}, u32[]{:S(2)}) copy-start(bf16[128,1024]{1,0:T(8,128)(2,1)} %param.27) | copy-start | bytes 786436
  650.3 33.8 %copy-start.24 = (f32[128]{0:T(128)S(1)}, f32[128]{0:T(128)}, u32[]{:S(2)}) copy-start(f32[128]{0:T(128)} %copy-done.23) | copy-start | bytes 1540
  650.3 67.6 %all-reduce.18.cloned.1.call-start = ((), (), s32[]{:S(2)}) async-start(), calls=%async_computation.7 | async-start | bytes 524288 | tf_op jit(solution)/shard_map/psum | solution.py:196
  656.5 119.1 %all-reduce.22.cloned.1.call-start = ((), (), s32[]{:S(2)}) async-start(), calls=%async_computation.9 | async-start | bytes 1048576 | tf_op jit(solution)/shard_map/psum | solution.py:244
  721.7 9.7 copy-start.22
  725.1 9.8 copy-start.17
  733.6 9.6 copy-start.10
  736.8 8.2 copy-start.7
  739.4 337.8 %reduce-scatter.2.cloned.1.call-start = ((), (), s32[]{:S(2)}) async-start(), calls=%async_computation.10 | async-start | bytes 35143680 | tf_op jit(solution)/shard_map/reduce_scatter | solution.py:253
  760.3 16.6 %copy-start.19 = (f32[1024]{0:T(1024)S(1)}, f32[1024]{0:T(1024)}, u32[]{:S(2)}) copy-start(f32[1024]{0:T(1024)} %get-tuple-element.13) | copy-start | bytes 12292
  760.3 16.6 %copy-start.25 = (f32[64]{0:T(128)S(1)}, f32[64]{0:T(128)}, u32[]{:S(2)}) copy-start(f32[64]{0:T(128)} %get-tuple-element.19) | copy-start | bytes 772
  (12 other events, 47.8 us)
Sparse Core Ops, SparseCore 0:
  11.3 68.3 all-gather.5
  83.1 62.7 all-gather.7
  382.3 28.9 all-reduce.15
  414.9 73.8 all-gather.11
  492.3 71.3 all-gather.9
  567.3 71.3 all-gather.13
  650.4 33.6 all-reduce.19
  687.1 30.7 all-reduce.17
  739.5 36.1 all-reduce.21
  781.9 295.2 reduce-scatter.1
where the time goes:
time: 1090 us
  blocking collectives  535 us (49%)
  waiting for transfers between devices  433 us (40%)
  matrix products  64.5 us (6%)
  other arithmetic  19.2 us (2%)
  local copies, waits for them, and re-layouts  18.9 us (2%)
  between operations  17.3 us (2%)
    unnamed x2, blocking collectives  348 us
    reduce_scatter x1, waiting for transfers between devices, on_device(): lax.psum_scatter(jnp.concatenate([jnp.concatenate([tr_matmul(hidden_one,...  114 us
    all_gather x1, blocking collectives, on_device(): lax.all_gather(shards[2], 'fsdp', axis=0, tiled=True)  91.7 us
    all_gather x1, blocking collectives, on_device(): lax.all_gather(shards[1], 'fsdp', axis=0, tiled=True)  89.9 us
    all_gather x1, waiting for transfers between devices, on_device(): lax.all_gather(shards[4], 'fsdp', axis=0, tiled=True)  75.6 us
    all_gather x1, waiting for transfers between devices, on_device(): lax.all_gather(shards[6], 'fsdp', axis=1, tiled=True)  70.8 us
    all_gather x1, waiting for transfers between devices, on_device(): lax.all_gather(shards[3], 'fsdp', axis=0, tiled=True)  70.8 us
    psum x1, waiting for transfers between devices, on_device(): lax.psum(matmul(activation, full_down).astype(jnp.bfloat16), 'tensor')  31.4 us
  transfers between devices with their start and end apart: 10, of which 8 were waited for; matrix products, arithmetic and copies ran while one was open for 6% of the time, Pallas kernels for 0%

commit v1 on v0

v1 whole, which is shorter than its diff:
```python
import jax
import jax.numpy as jnp
from jax import lax
from jax.sharding import Mesh
from jax.sharding import PartitionSpec as P

epsilon = 1e-05
rope_base = 1000000.0
bf16 = jnp.bfloat16
f32 = jnp.float32
FSDP = ("z", "h", "y", "c")
BITS = {
    "c": ("c", 2, 1),
    "ya": ("y", 4, 1),
    "yb": ("y", 4, 3),
    "za": ("z", 4, 1),
    "zb": ("z", 4, 3),
    "h": ("h", 2, 1),
}


def matmul(matrix, second):
    return jnp.dot(matrix, second, preferred_element_type=f32)


def matmul_tr(matrix, second):
    return lax.dot_general(matrix, second, (((1,), (1,)), ((), ())), preferred_element_type=f32)


def tr_matmul(matrix, second):
    return lax.dot_general(matrix, second, (((0,), (0,)), ((), ())), preferred_element_type=f32)


def contract(pattern, matrix, second):
    return jnp.einsum(pattern, matrix, second, preferred_element_type=f32)


def normalize(vector):
    inverse = lax.rsqrt(jnp.mean(vector * vector, axis=-1, keepdims=True) + epsilon)
    return (vector * inverse, inverse)


def norm_back(grad_in, normed, inverse):
    return inverse * (grad_in - normed * jnp.mean(grad_in * normed, axis=-1, keepdims=True))


def rotate(vector):
    half_size = vector.shape[-1] // 2
    return jnp.concatenate([-vector[..., half_size:], vector[..., :half_size]], axis=-1)


def rotate_back(vector):
    half_size = vector.shape[-1] // 2
    return jnp.concatenate([vector[..., half_size:], -vector[..., :half_size]], axis=-1)


def tables(segment, head_size):
    row_count = segment.shape[0]
    row_index = jnp.arange(row_count, dtype=jnp.int32)
    same_segment = segment[:, None] == segment[None, :]
    first_row = jnp.min(jnp.where(same_segment, row_index[None, :], row_count), axis=1)
    position = (row_index - first_row).astype(f32)
    allowed = same_segment & (row_index[None, :] <= row_index[:, None])
    half_size = head_size // 2
    frequency = jnp.power(rope_base, -2.0 * jnp.arange(half_size, dtype=f32) / head_size)
    phase_angle = position[:, None] * frequency[None, :]
    phase_angle = jnp.concatenate([phase_angle, phase_angle], axis=1)
    return (allowed, jnp.cos(phase_angle)[:, None, :], jnp.sin(phase_angle)[:, None, :])


def head_prep(raw_heads, head_gain, cos_table, sin_table):
    unit_heads, inverse = normalize(raw_heads)
    scaled = unit_heads * head_gain
    return (scaled * cos_table + rotate(scaled) * sin_table, unit_heads, inverse)


def head_back(grad_in, unit_heads, inverse, head_gain, cos_table, sin_table):
    grad_scaled = grad_in * cos_table + rotate_back(grad_in * sin_table)
    gain_grad = jnp.sum(grad_scaled * unit_heads, axis=(0, 1))
    return (norm_back(grad_scaled * head_gain, unit_heads, inverse), gain_grad)


def score_block(query_heads, key_heads, allowed):
    row_count, head_count, head_size = query_heads.shape
    kv_count = key_heads.shape[1]
    query_groups = query_heads.reshape(row_count, kv_count, head_count // kv_count, head_size)
    scores = contract("ikgd,jkd->kgij", query_groups, key_heads) * head_size ** (-0.5)
    return (query_groups, jnp.where(allowed, scores, -1e30))


def attend(query_heads, key_heads, value_heads, allowed):
    row_count, head_count, head_size = query_heads.shape
    query_groups, masked = score_block(query_heads, key_heads, allowed)
    row_max = jnp.max(masked, axis=-1, keepdims=True)
    exp_scores = jnp.exp(masked - row_max)
    denominator = jnp.sum(exp_scores, axis=-1, keepdims=True)
    log_total = row_max + jnp.log(denominator)
    attn_weights = (exp_scores / denominator).astype(bf16)
    mixed = contract("kgij,jkd->ikgd", attn_weights, value_heads).astype(bf16)
    return (mixed.reshape(row_count, head_count * head_size), log_total)


def attend_back(query_heads, key_heads, value_heads, attended, grad_attended, log_total, allowed):
    row_count, head_count, head_size = query_heads.shape
    kv_count = key_heads.shape[1]
    group_size = head_count // kv_count
    query_groups, masked = score_block(query_heads, key_heads, allowed)
    prob = jnp.exp(masked - log_total)
    prob_low = prob.astype(bf16)
    grad_groups = grad_attended.reshape(row_count, kv_count, group_size, head_size)
    out_groups = attended.reshape(row_count, kv_count, group_size, head_size)
    row_delta = jnp.sum(grad_groups.astype(f32) * out_groups.astype(f32), axis=-1)
    row_delta = jnp.transpose(row_delta, (1, 2, 0))[..., None]
    grad_kv_value = contract("kgij,ikgd->jkd", prob_low, grad_groups)
    grad_prob = contract("ikgd,jkd->kgij", grad_groups, value_heads)
    grad_scores = (prob * (grad_prob - row_delta) * head_size ** (-0.5)).astype(bf16)
    grad_query = contract("kgij,jkd->ikgd", grad_scores, key_heads).reshape(
        row_count, head_count, head_size
    )
    grad_key = contract("kgij,ikgd->jkd", grad_scores, query_groups)
    return (grad_query, grad_key, grad_kv_value)


def swap(array, bit):
    axis, size, flip = BITS[bit]
    return lax.ppermute(array, axis, [(i, i ^ flip) for i in range(size)])


def swap_pair(low):
    return lax.ppermute(low, "t", [(0, 1), (1, 0)])


def add_pair(low, other):
    return low.astype(f32) + other.astype(f32)


def absolute_rows(width):
    block = width // 64
    r = lax.broadcasted_iota(jnp.int32, (1, width), 1)
    k = r % block
    bits = r // block
    h, zb, za, yb, ya, c = ((bits >> i) & 1 for i in range(6))
    z_at = lax.axis_index("z") ^ za ^ (3 * zb)
    y_at = lax.axis_index("y") ^ ya ^ (3 * yb)
    h_at = lax.axis_index("h") ^ h
    c_at = lax.axis_index("c") ^ c
    return (((z_at * 2 + h_at) * 4 + y_at) * 2 + c_at) * block + k


ORDERS = (
    ("ya", "yb", "za", "zb", "h"),
    ("yb", "ya", "zb", "za", "h"),
    ("za", "zb", "ya", "yb", "h"),
    ("zb", "za", "yb", "ya", "h"),
)
INNER = ("ya", "yb", "za", "zb", "h")


def exchange(arrays, bits, after=()):
    arrays = lax.optimization_barrier(tuple(arrays) + tuple(after))[: len(arrays)]
    return [swap(a.reshape(-1, a.shape[-1]), b).reshape(a.shape) for a, b in zip(arrays, bits)]


def join(first, second):
    both = lax.optimization_barrier(tuple(first) + tuple(second))
    return list(both[: len(first)]), list(both[len(first) :])


class Gather:
    def __init__(self, pack, order):
        self.held = pack
        self.order = order[::-1]
        self.names = []

    def take(self, got):
        bit = self.order[len(self.names)]
        self.names = [n for n in INNER if n in self.names or n == bit]
        self.held = jnp.stack([self.held, got], axis=self.names.index(bit))

    @property
    def bit(self):
        return self.order[len(self.names)]

    def rows(self):
        return self.held.reshape(-1, self.held.shape[-1])


class Reduce:
    def __init__(self, order):
        self.order = order
        self.names = list(INNER)

    def begin(self, own, got):
        held = (own + got.astype(f32)).astype(bf16)
        rows = held.shape[0] // 2 ** len(self.names)
        self.held = held.reshape((2,) * len(self.names) + (rows, held.shape[1]))

    @property
    def bit(self):
        return self.order[len(INNER) - len(self.names)]

    def give(self):
        return lax.index_in_dim(self.held, 1, self.names.index(self.bit), keepdims=False)

    def take(self, got):
        own = lax.index_in_dim(self.held, 0, self.names.index(self.bit), keepdims=False)
        self.names.remove(self.bit)
        self.held = own.astype(f32) + got.astype(f32)
        if self.names:
            self.held = self.held.astype(bf16)


def advance(streams, after=()):
    gots = exchange([s.give() for s in streams], [s.bit for s in streams], after)
    for stream, got in zip(streams, gots):
        stream.take(got)


def tie(streams, values):
    held, values = join([s.held for s in streams], values)
    for stream, array in zip(streams, held):
        stream.held = array
    return values


def on_device(
    tokens,
    segment,
    w_query,
    w_key,
    w_value,
    w_output,
    w_gate,
    w_up,
    w_down,
    norm_attn,
    norm_ffn,
    norm_query,
    norm_key,
    cotangent,
):
    rows_own, q_width = w_query.shape
    kv_width = w_key.shape[1]
    ff_width = w_gate.shape[1]
    row_count, width = tokens.shape
    half = width // 2
    head_size = 64
    gain_block = jnp.concatenate(
        [
            norm_attn[:, None],
            norm_ffn[:, None],
            jnp.broadcast_to(norm_query[:, None], (rows_own, 1)),
            jnp.broadcast_to(norm_key[:, None], (rows_own, 1)),
            jnp.zeros((rows_own, 124), bf16),
        ],
        axis=1,
    )
    attn = [
        Gather(jnp.concatenate([w_query, w_key], axis=1), ORDERS[0]),
        Gather(jnp.concatenate([w_value, w_output.T, gain_block], axis=1), ORDERS[2]),
    ]
    ffn = [
        Gather(w_gate, ORDERS[1]),
        Gather(w_up, ORDERS[3]),
        Gather(w_down.T, ORDERS[2]),
    ]
    for step in range(len(INNER)):
        ahead = [g.held for g in attn]
        gots = exchange(ahead, [g.bit for g in attn])
        late = exchange([g.held for g in ffn], [g.bit for g in ffn], ahead)
        for g, got in zip(attn, gots):
            g.take(got)
        for g, got in zip(ffn, late):
            g.take(got)
    mine = [g.rows() for g in attn]
    theirs = exchange(mine, ["c", "c"])
    w_qk = jnp.concatenate([mine[0], theirs[0]], axis=0)
    w_vog = jnp.concatenate([mine[1], theirs[1]], axis=0)
    mine = [g.rows() for g in ffn]
    theirs = exchange(mine, ["c", "c", "c"])
    gate_own, up_own, down_own = mine
    gate_other, up_other, down_other = theirs

    absolute = absolute_rows(width)
    relative = (
        lax.broadcasted_iota(jnp.int32, (width, width), 0) == absolute
    ).astype(bf16)
    head_rows = (
        lax.broadcasted_iota(jnp.int32, (head_size, width), 0) * rows_own == absolute
    ).astype(bf16)
    tokens = matmul(tokens, relative).astype(bf16)
    cotangent = matmul(cotangent, relative).astype(bf16)
    cot_own, cot_other = cotangent[:, :half], cotangent[:, half:]

    gains = w_vog[:, kv_width + q_width :].T
    gain_heads = matmul_tr(gains[:8], head_rows)
    gains = gains[:8].astype(f32)
    gain_attn, gain_ffn = gains[0], gains[1]
    gain_query, gain_key = gain_heads[2], gain_heads[3]
    w_v = w_vog[:, :kv_width]
    w_o = w_vog[:, kv_width : kv_width + q_width]

    head_count = q_width // head_size
    kv_count = kv_width // head_size
    allowed, cos_table, sin_table = tables(segment, head_size)
    inputs = tokens.astype(f32)
    normed_one, inv_one = normalize(inputs)
    hidden_one = (normed_one * gain_attn).astype(bf16)
    qk_raw = matmul(hidden_one, w_qk)
    query_raw = qk_raw[:, :q_width].reshape(row_count, head_count, head_size)
    key_raw = qk_raw[:, q_width:].reshape(row_count, kv_count, head_size)
    value_heads = matmul(hidden_one, w_v).astype(bf16).reshape(row_count, kv_count, head_size)
    query_rot, query_unit, query_inv = head_prep(query_raw, gain_query, cos_table, sin_table)
    key_rot, key_unit, key_inv = head_prep(key_raw, gain_key, cos_table, sin_table)
    query_heads = query_rot.astype(bf16)
    key_heads = key_rot.astype(bf16)
    attended, log_total = attend(query_heads, key_heads, value_heads, allowed)
    low = matmul_tr(attended, w_o).astype(bf16)
    residual = inputs + add_pair(low, swap_pair(low))
    normed_two, inv_two = normalize(residual)
    hidden_two = (normed_two * gain_ffn).astype(bf16)
    hid_own, hid_other = hidden_two[:, :half], hidden_two[:, half:]
    gate_pre = matmul(hid_own, gate_own) + matmul(hid_other, gate_other)
    up_pre = matmul(hid_own, up_own) + matmul(hid_other, up_other)
    sigmoid_gate = jax.nn.sigmoid(gate_pre)
    activation = (gate_pre * sigmoid_gate * up_pre).astype(bf16)
    grad_act = matmul(cot_own, down_own) + matmul(cot_other, down_other)
    grad_gate_pre = (
        grad_act * up_pre * sigmoid_gate * (1.0 + gate_pre * (1.0 - sigmoid_gate))
    ).astype(bf16)
    grad_up_pre = (grad_act * gate_pre * sigmoid_gate).astype(bf16)

    low = jnp.concatenate(
        [
            matmul_tr(grad_gate_pre, gate_own) + matmul_tr(grad_up_pre, up_own),
            matmul_tr(grad_gate_pre, gate_other) + matmul_tr(grad_up_pre, up_other),
        ],
        axis=1,
    ).astype(bf16)
    other = swap_pair(low)
    third = 2 * ff_width // 3
    grad_pre = jnp.concatenate([grad_gate_pre, grad_up_pre], axis=1)
    rights = [grad_pre[:, i * third : (i + 1) * third] for i in range(3)] + [activation]
    out_left = [hid_other] * 3 + [cot_other]
    own_left = [hid_own] * 3 + [cot_own]
    fed = [Reduce(ORDERS[i]) for i in (1, 2, 3, 0)]
    gots = exchange(
        [tr_matmul(a, b).astype(bf16) for a, b in zip(out_left, rights)], ["c"] * 4, [low]
    )
    for stream, a, b, got in zip(fed, own_left, rights, gots):
        stream.begin(tr_matmul(a, b), got)
    (low, other) = tie(fed, [low, other])

    advance(fed)
    grad_hidden_two = add_pair(low, other)
    grad_norm_ffn = jnp.sum(grad_hidden_two * normed_two, axis=0)
    grad_residual = cotangent.astype(f32) + norm_back(
        grad_hidden_two * gain_ffn, normed_two, inv_two
    )
    grad_res_low = grad_residual.astype(bf16)
    grad_attended = matmul(grad_res_low, w_o).astype(bf16)
    grads = attend_back(
        query_heads, key_heads, value_heads, attended, grad_attended, log_total, allowed
    )
    grads = tie(fed, list(grads) + [activation])
    activation = grads.pop()

    advance(fed)
    grad_q_rot, grad_k_rot, grad_kv_value = grads
    grad_q_raw, part_norm_query = head_back(
        grad_q_rot, query_unit, query_inv, gain_query, cos_table, sin_table
    )
    grad_k_raw, part_norm_key = head_back(
        grad_k_rot, key_unit, key_inv, gain_key, cos_table, sin_table
    )
    query_low = grad_q_raw.reshape(row_count, head_count * head_size).astype(bf16)
    key_low = grad_k_raw.reshape(row_count, kv_count * head_size).astype(bf16)
    value_low = grad_kv_value.reshape(row_count, kv_count * head_size).astype(bf16)
    low_out = jnp.concatenate(
        [matmul_tr(activation, down_own), matmul_tr(activation, down_other)], axis=1
    ).astype(bf16)
    query_low, key_low, value_low, low_out = tie(fed, [query_low, key_low, value_low, low_out])

    advance(fed)
    partial_one = matmul_tr(jnp.concatenate([query_low, key_low], axis=1), w_qk) + matmul_tr(
        value_low, w_v
    )
    low = partial_one.astype(bf16)
    other = swap_pair(low)
    other_out = swap_pair(low_out)
    head_gains = jnp.stack([part_norm_query, part_norm_key]).astype(bf16)
    gain_rows = jnp.concatenate(
        [
            jnp.sum(partial_one * normed_one, axis=0)[None],
            0.5 * grad_norm_ffn[None],
            matmul(head_gains, head_rows),
            jnp.zeros((124, width), f32),
        ],
        axis=0,
    ).astype(bf16)
    eye = (
        lax.broadcasted_iota(jnp.int32, (128, 128), 0)
        == lax.broadcasted_iota(jnp.int32, (128, 128), 1)
    ).astype(bf16)
    kv_low = jnp.concatenate([key_low, value_low], axis=1)

    def late_parts(at):
        side = slice(at * half, (at + 1) * half)
        return [
            jnp.concatenate(
                [tr_matmul(hidden_one[:, side], query_low), tr_matmul(gain_rows[:, side], eye)],
                axis=1,
            ),
            tr_matmul(hidden_one[:, side], kv_low),
            tr_matmul(grad_res_low[:, side], attended),
        ]

    late = [Reduce(ORDERS[i]) for i in (0, 2, 1)]
    gots = exchange([p.astype(bf16) for p in late_parts(1)], ["c"] * 3)
    for stream, own, got in zip(late, late_parts(0), gots):
        stream.begin(own, got)
    low, other, low_out, other_out = tie(fed + late, [low, other, low_out, other_out])

    advance(fed + late)
    grad_hidden_one = add_pair(low, other)
    grad_tokens = (
        grad_residual + norm_back(grad_hidden_one * gain_attn, normed_one, inv_one)
    ).astype(bf16)
    grad_tokens = matmul_tr(grad_tokens, relative).astype(bf16)
    block_out = (residual + add_pair(low_out, other_out)).astype(bf16)
    block_out = matmul_tr(block_out, relative).astype(bf16)
    advance(late + fed)
    advance(late)
    advance(late)
    advance(late)
    owned_gain = late[0].held[:, q_width:]
    owned_gain = owned_gain + swap_pair(owned_gain)
    owned_gu = jnp.concatenate([s.held for s in fed[:3]], axis=1)
    return (
        block_out,
        grad_tokens,
        late[0].held[:, :q_width],
        late[1].held[:, :kv_width],
        late[1].held[:, kv_width:],
        late[2].held.T,
        owned_gu[:, :ff_width],
        owned_gu[:, ff_width:],
        fed[3].held.T,
        owned_gain[:, 0],
        owned_gain[:, 1],
        owned_gain[:1, 2],
        owned_gain[:1, 3],
    )


def solution(mesh):
    fine = Mesh(mesh.devices.reshape(4, 2, 4, 2, 2), ("z", "h", "y", "c", "t"))
    weight = P(FSDP, "t")
    weight_tr = P("t", FSDP)
    rows = P(FSDP, None)
    vector = P(FSDP)
    return jax.shard_map(
        on_device,
        mesh=fine,
        in_specs=(
            rows,
            vector,
            weight,
            weight,
            weight,
            weight_tr,
            weight,
            weight,
            weight_tr,
            vector,
            vector,
            vector,
            vector,
            rows,
        ),
        out_specs=(
            rows,
            rows,
            weight,
            weight,
            weight,
            weight_tr,
            weight,
            weight,
            weight_tr,
            vector,
            vector,
            vector,
            vector,
        ),
        check_vma=False,
    )
```

time: 1090 us -> 303 us (0.28)
  blocking collectives: 535 us -> 0 us
  waiting for transfers between devices: 433 us -> 119 us
  starting transfers between devices: 0.57 us -> 92.4 us
  matrix products: 64.5 us -> 34.7 us
  between operations: 17.3 us -> 4.18 us
    unnamed x2 -> x0, blocking collectives: 348 us -> none
    all_gather x5 -> x0, waiting for transfers between devices: 217 us -> none  [the longest x1 75.6 us: on_device(): lax.all_gather(shards[4], 'fsdp', axis=0, tiled=True)]
    all_gather x2 -> x0, blocking collectives: 182 us -> none  [the longest x1 91.7 us: on_device(): lax.all_gather(shards[2], 'fsdp', axis=0, tiled=True)]
    ppermute x0 -> x77, waiting for transfers between devices: none -> 119 us  [the longest x72 110 us: swap(): return lax.ppermute(array, axis, [(i, i ^ flip) for i in range(size)])]
    reduce_scatter x1 -> x0, waiting for transfers between devices: 114 us -> none  [on_device(): lax.psum_scatter(jnp.concatenate([jnp.concatenate([tr_matmul(hidden_one,...]
    psum x4 -> x0, waiting for transfers between devices: 99 us -> none  [the longest x1 31.4 us: on_device(): lax.psum(matmul(activation, full_down).astype(jnp.bfloat16), 'tensor')]
    ppermute x0 -> x77, starting transfers between devices: none -> 92.4 us  [the longest x72 87.9 us: swap(): return lax.ppermute(array, axis, [(i, i ^ flip) for i in range(size)])]
    dot_general x13 -> x18, matrix products: 22.9 us -> 9.78 us  [the longest x12 7.69 us: matmul(): return jnp.dot(matrix, second, preferred_element_type=f32)]
  transfers between devices with their start and end apart: 10 -> 77, of which waited for: 8 -> 43; matrix products, arithmetic and copies ran while one was open for 6% -> 16% of each run, Pallas kernels for 0% -> 0%
where the time goes in v1:
time: 303 us; the launch traced here: 298 us
  waiting for transfers between devices  119 us (39%)
  starting transfers between devices  92.4 us (30%)
  matrix products  34.7 us (11%)
  local copies, waits for them, and re-layouts  24.4 us (8%)
  other arithmetic  24.3 us (8%)
  between operations  4.18 us (1%)
    ppermute x72, waiting for transfers between devices, swap(): return lax.ppermute(array, axis, [(i, i ^ flip) for i in range(size)])  110 us
    ppermute x72, starting transfers between devices, swap(): return lax.ppermute(array, axis, [(i, i ^ flip) for i in range(size)])  87.9 us
    dot_general x12, matrix products, matmul_tr(): lax.dot_general(matrix, second, (((1,), (1,)), ((), ())), preferred_eleme...  12.8 us
    dot_general x16, matrix products, tr_matmul(): lax.dot_general(matrix, second, (((0,), (0,)), ((), ())), preferred_eleme...  12.1 us
    another operation x25, other arithmetic, take(): self.held = jnp.stack([self.held, got], axis=self.names.index(bit))  9.65 us
    ppermute x5, waiting for transfers between devices, swap_pair(): return lax.ppermute(low, 't', [(0, 1), (1, 0)])  8.77 us
    unnamed x144, local copies, waits for them, and re-layouts  8.69 us
    dot_general x12, matrix products, matmul(): return jnp.dot(matrix, second, preferred_element_type=f32)  7.69 us
  transfers between devices with their start and end apart: 77, of which 43 were waited for; matrix products, arithmetic and copies ran while one was open for 16% of the time, Pallas kernels for 0%

profile of v1, /device:TPU:0, one launch (start us, length us, event | category | flops | bytes accessed | tf_op | source)
XLA Modules:
  0.0 298.5 jit_solution(2046979772471813010)
XLA Ops:
  5.8 3.2 %collective-permute-start.1 = (bf16[16,768]{1,0:T(8,128)(2,1)S(1)}, bf16[16,768]{1,0:T(8,128)(2,1)S(1)}, u32[]{:S(2)}, u32[]{:S(2)}) collective-permute-start(bf16[16,768]{1,0:T(8,128)(2,1)S(1)} %constant_dynamic-update-slice_fusion), channel_id=1, source_target_pairs={{0,16},{16,0},{1,17},{17,1},{2,18},{18,2},{3,19},{19,3},{4,20},{20... | collective-permute-start | bytes 73736 | tf_op jit(solution)/shard_map/ppermute | solution.py:126
  9.4 3.1 %collective-permute-start.13 = (bf16[16,2304]{1,0:T(8,128)(2,1)}, bf16[16,2304]{1,0:T(8,128)(2,1)S(1)}, u32[]{:S(2)}, u32[]{:S(2)}) collective-permute-start(bf16[16,2304]{1,0:T(8,128)(2,1)} %bitcast.676), channel_id=1, source_target_pairs={{0,16},{16,0},{1,17},{17,1},{2,18},{18,2},{3,19},{19,3},{4,20},{20... | collective-permute-start | bytes 221192 | tf_op jit(solution)/shard_map/ppermute | solution.py:126
  12.9 3.1 %collective-permute-start.15 = (bf16[16,2304]{1,0:T(8,128)(2,1)}, bf16[16,2304]{1,0:T(8,128)(2,1)S(1)}, u32[]{:S(2)}, u32[]{:S(2)}) collective-permute-start(bf16[16,2304]{1,0:T(8,128)(2,1)} %param.21), channel_id=1, source_target_pairs={{0,16},{16,0},{1,17},{17,1},{2,18},{18,2},{3,19},{19,3},{4,20},{20... | collective-permute-start | bytes 221192 | tf_op jit(solution)/shard_map/ppermute | solution.py:126
  17.8 4.1 %collective-permute-start.3 = (bf16[32,768]{1,0:T(8,128)(2,1)S(1)}, bf16[32,768]{1,0:T(8,128)(2,1)S(1)}, u32[]{:S(2)}, u32[]{:S(2)}) collective-permute-start(bf16[32,768]{1,0:T(8,128)(2,1)S(1)} %bitcast.689), channel_id=1, source_target_pairs={{0,96},{32,64},{64,32},{96,0},{1,97},{33,65},{65,33},{97,1},{2,98}... | collective-permute-start | bytes 147464 | tf_op jit(solution)/shard_map/ppermute | solution.py:126
  22.0 3.0 %collective-permute-start.2 = (bf16[32,896]{1,0:T(8,128)(2,1)S(1)}, bf16[32,896]{1,0:T(8,128)(2,1)S(1)}, u32[]{:S(2)}, u32[]{:S(2)}) collective-permute-start(bf16[32,896]{1,0:T(8,128)(2,1)S(1)} %bitcast.686), channel_id=1, source_target_pairs={{0,12},{4,8},{8,4},{12,0},{1,13},{5,9},{9,5},{13,1},{2,14},{6,10},... | collective-permute-start | bytes 172040 | tf_op jit(solution)/shard_map/ppermute | solution.py:126
  29.6 3.0 %collective-permute-start.16 = (bf16[32,2304]{1,0:T(8,128)(2,1)S(1)}, bf16[32,2304]{1,0:T(8,128)(2,1)S(1)}, u32[]{:S(2)}, u32[]{:S(2)}) collective-permute-start(bf16[32,2304]{1,0:T(8,128)(2,1)S(1)} %bitcast.651), channel_id=1, source_target_pairs={{0,12},{4,8},{8,4},{12,0},{1,13},{5,9},{9,5},{13,1},{2,14},{6,10},... | collective-permute-start | bytes 442376 | tf_op jit(solution)/shard_map/ppermute | solution.py:126
  34.7 4.3 %collective-permute-done.4 = bf16[64,896]{1,0:T(8,128)(2,1)S(1)} collective-permute-done((bf16[64,896]{1,0:T(8,128)(2,1)S(1)}, bf16[64,896]{1,0:T(8,128)(2,1)S(1)}, u32[]{:S(2)}, u32[]{:S(2)}) %collective-permute-start.4) | collective-permute-done | bytes 114720 | tf_op jit(solution)/shard_map/ppermute | solution.py:126
  39.6 3.1 %collective-permute-start.21 = (bf16[64,2304]{1,0:T(8,128)(2,1)S(1)}, bf16[64,2304]{1,0:T(8,128)(2,1)S(1)}, u32[]{:S(2)}, u32[]{:S(2)}) collective-permute-start(bf16[64,2304]{1,0:T(8,128)(2,1)S(1)} %bitcast.620), channel_id=1, source_target_pairs={{0,12},{4,8},{8,4},{12,0},{1,13},{5,9},{9,5},{13,1},{2,14},{6,10},... | collective-permute-start | bytes 884744 | tf_op jit(solution)/shard_map/ppermute | solution.py:126
  43.4 3.1 %collective-permute-start.20 = (bf16[64,2304]{1,0:T(8,128)(2,1)S(1)}, bf16[64,2304]{1,0:T(8,128)(2,1)S(1)}, u32[]{:S(2)}, u32[]{:S(2)}) collective-permute-start(bf16[64,2304]{1,0:T(8,128)(2,1)S(1)} %bitcast.622), channel_id=1, source_target_pairs={{0,96},{32,64},{64,32},{96,0},{1,97},{33,65},{65,33},{97,1},{2,98}... | collective-permute-start | bytes 884744 | tf_op jit(solution)/shard_map/ppermute | solution.py:126
  49.2 7.3 %collective-permute-done.19 = bf16[64,2304]{1,0:T(8,128)(2,1)S(1)} collective-permute-done((bf16[64,2304]{1,0:T(8,128)(2,1)S(1)}, bf16[64,2304]{1,0:T(8,128)(2,1)S(1)}, u32[]{:S(2)}, u32[]{:S(2)}) %collective-permute-start.19) | collective-permute-done | bytes 294944 | tf_op jit(solution)/shard_map/ppermute | solution.py:126
  57.8 6.3 %collective-permute-done.9 = bf16[256,768]{1,0:T(8,128)(2,1)S(1)} collective-permute-done((bf16[256,768]{1,0:T(8,128)(2,1)S(1)}, bf16[256,768]{1,0:T(8,128)(2,1)S(1)}, u32[]{:S(2)}, u32[]{:S(2)}) %collective-permute-start.9) | collective-permute-done | bytes 393248 | tf_op jit(solution)/shard_map/ppermute | solution.py:126
  75.4 10.4 %collective-permute-start.25 = (bf16[256,2304]{1,0:T(8,128)(2,1)}, bf16[256,2304]{1,0:T(8,128)(2,1)}, u32[]{:S(2)}, u32[]{:S(2)}) collective-permute-start(bf16[256,2304]{1,0:T(8,128)(2,1)} %bitcast.89), channel_id=1, source_target_pairs={{0,32},{32,0},{64,96},{96,64},{1,33},{33,1},{65,97},{97,65},{2,34}... | collective-permute-start | bytes 3538952 | tf_op jit(solution)/shard_map/ppermute | solution.py:126
  94.2 5.5 %collective-permute-done.27 = bf16[256,2304]{1,0:T(8,128)(2,1)} collective-permute-done((bf16[256,2304]{1,0:T(8,128)(2,1)}, bf16[256,2304]{1,0:T(8,128)(2,1)}, u32[]{:S(2)}, u32[]{:S(2)}) %collective-permute-start.27) | collective-permute-done | bytes 1179680 | tf_op jit(solution)/shard_map/ppermute | solution.py:126
  104.4 4.7 %collective-permute-done.25 = bf16[256,2304]{1,0:T(8,128)(2,1)} collective-permute-done((bf16[256,2304]{1,0:T(8,128)(2,1)}, bf16[256,2304]{1,0:T(8,128)(2,1)}, u32[]{:S(2)}, u32[]{:S(2)}) %collective-permute-start.25) | collective-permute-done | bytes 1179680 | tf_op jit(solution)/shard_map/ppermute | solution.py:126
  114.1 6.9 %collective-permute-done.12 = bf16[128,1024]{0,1:T(8,128)(2,1)S(1)} collective-permute-done((bf16[128,1024]{0,1:T(8,128)(2,1)S(1)}, bf16[128,1024]{0,1:T(8,128)(2,1)S(1)}, u32[]{:S(2)}, u32[]{:S(2)}) %collective-permute-start.12) | collective-permute-done | bytes 262176 | tf_op jit(solution)/shard_map/ppermute | solution.py:130
  136.8 3.9 %collective-permute-done.31 = bf16[512,1536]{1,0:T(8,128)(2,1)S(1)} collective-permute-done((bf16[512,1536]{1,0:T(8,128)(2,1)S(1)}, bf16[512,1536]{1,0:T(8,128)(2,1)S(1)}, u32[]{:S(2)}, u32[]{:S(2)}) %collective-permute-start.31) | collective-permute-done | bytes 1572896 | tf_op jit(solution)/shard_map/ppermute | solution.py:126
  159.4 3.0 %collective-permute-start.38 = (bf16[256,1536]{1,0:T(8,128)(2,1)S(1)}, bf16[256,1536]{1,0:T(8,128)(2,1)S(1)}, u32[]{:S(2)}, u32[]{:S(2)}) collective-permute-start(bf16[256,1536]{1,0:T(8,128)(2,1)S(1)} %bitcast.590), channel_id=1, source_target_pairs={{0,96},{32,64},{64,32},{96,0},{1,97},{33,65},{65,33},{97,1},{2,98}... | collective-permute-start | bytes 2359304 | tf_op jit(solution)/shard_map/ppermute | solution.py:126
  162.8 12.3 %collective-permute-done.37 = bf16[256,1536]{1,0:T(8,128)(2,1)S(1)} collective-permute-done((bf16[256,1536]{1,0:T(8,128)(2,1)S(1)}, bf16[256,1536]{1,0:T(8,128)(2,1)S(1)}, u32[]{:S(2)}, u32[]{:S(2)}) %collective-permute-start.37) | collective-permute-done | bytes 786464 | tf_op jit(solution)/shard_map/ppermute | solution.py:126
  176.7 3.2 %collective-permute-done.38 = bf16[256,1536]{1,0:T(8,128)(2,1)S(1)} collective-permute-done((bf16[256,1536]{1,0:T(8,128)(2,1)S(1)}, bf16[256,1536]{1,0:T(8,128)(2,1)S(1)}, u32[]{:S(2)}, u32[]{:S(2)}) %collective-permute-start.38) | collective-permute-done | bytes 786464 | tf_op jit(solution)/shard_map/ppermute | solution.py:126
  180.1 9.6 %collective-permute-done.39 = bf16[256,2304]{1,0:T(8,128)(2,1)S(1)} collective-permute-done((bf16[256,2304]{1,0:T(8,128)(2,1)S(1)}, bf16[256,2304]{1,0:T(8,128)(2,1)S(1)}, u32[]{:S(2)}, u32[]{:S(2)}) %collective-permute-start.39) | collective-permute-done | bytes 1179680 | tf_op jit(solution)/shard_map/ppermute | solution.py:126
  196.8 4.6 %collective-permute-done.42 = bf16[128,1536]{1,0:T(8,128)(2,1)S(1)} collective-permute-done((bf16[128,1536]{1,0:T(8,128)(2,1)S(1)}, bf16[128,1536]{1,0:T(8,128)(2,1)S(1)}, u32[]{:S(2)}, u32[]{:S(2)}) %collective-permute-start.42) | collective-permute-done | bytes 393248 | tf_op jit(solution)/shard_map/ppermute | solution.py:126
  203.6 5.3 %collective-permute-done.43 = bf16[128,2304]{1,0:T(8,128)(2,1)S(1)} collective-permute-done((bf16[128,2304]{1,0:T(8,128)(2,1)S(1)}, bf16[128,2304]{1,0:T(8,128)(2,1)S(1)}, u32[]{:S(2)}, u32[]{:S(2)}) %collective-permute-start.43) | collective-permute-done | bytes 589856 | tf_op jit(solution)/shard_map/ppermute | solution.py:126
  232.2 3.1 %fusion.34 = bf16[128,1024]{1,0:T(8,128)(2,1)} fusion(s32[1024]{0:T(1024)S(1)} %copy-done.62, bf16[128,1024]{0,1:T(8,128)(2,1)} %collective-permute-done.51, bf16[128,1024]{0,1:T(8,128)(2,1)} %get-tuple-element.191, f32[128,1024]{0,1:T(8,128)S(1)} %copy-done.18, f32[128]{0:T(128)S(1)} %broadcast_multiply_fusion.5, f32[1024]{0:T(1024)S(1)} %get-tuple-element.226, ...), kind=kOutput, calls=%fused_computation.55 | convolution fusion | flops 272236544 | bytes 2635776 | tf_op jit(solution)/shard_map/dot_general | solution.py:27
  243.6 3.1 %collective-permute-done.54 = bf16[256,512]{1,0:T(8,128)(2,1)S(1)} collective-permute-done((bf16[256,512]{1,0:T(8,128)(2,1)S(1)}, bf16[256,512]{1,0:T(8,128)(2,1)S(1)}, u32[]{:S(2)}, u32[]{:S(2)}) %collective-permute-start.54) | collective-permute-done | bytes 262176 | tf_op jit(solution)/shard_map/ppermute | solution.py:126
  (498 shorter events, 175.0 us)
Async XLA Ops:
  9.4 18.1 %collective-permute-start.13 = (bf16[16,2304]{1,0:T(8,128)(2,1)}, bf16[16,2304]{1,0:T(8,128)(2,1)S(1)}, u32[]{:S(2)}, u32[]{:S(2)}) collective-permute-start(bf16[16,2304]{1,0:T(8,128)(2,1)} %bitcast.676), channel_id=1, source_target_pairs={{0,16},{16,0},{1,17},{17,1},{2,18},{18,2},{3,19},{19,3},{4,20},{20... | collective-permute-start | bytes 221192 | tf_op jit(solution)/shard_map/ppermute | solution.py:126
  12.5 12.5 %collective-permute-start.14 = (bf16[16,2304]{1,0:T(8,128)(2,1)}, bf16[16,2304]{1,0:T(8,128)(2,1)S(1)}, u32[]{:S(2)}, u32[]{:S(2)}) collective-permute-start(bf16[16,2304]{1,0:T(8,128)(2,1)} %param.20), channel_id=1, source_target_pairs={{0,16},{16,0},{1,17},{17,1},{2,18},{18,2},{3,19},{19,3},{4,20},{20... | collective-permute-start | bytes 221192 | tf_op jit(solution)/shard_map/ppermute | solution.py:126
  43.4 13.2 %collective-permute-start.20 = (bf16[64,2304]{1,0:T(8,128)(2,1)S(1)}, bf16[64,2304]{1,0:T(8,128)(2,1)S(1)}, u32[]{:S(2)}, u32[]{:S(2)}) collective-permute-start(bf16[64,2304]{1,0:T(8,128)(2,1)S(1)} %bitcast.622), channel_id=1, source_target_pairs={{0,96},{32,64},{64,32},{96,0},{1,97},{33,65},{65,33},{97,1},{2,98}... | collective-permute-start | bytes 884744 | tf_op jit(solution)/shard_map/ppermute | solution.py:126
  47.6 16.5 %collective-permute-start.9 = (bf16[256,768]{1,0:T(8,128)(2,1)S(1)}, bf16[256,768]{1,0:T(8,128)(2,1)S(1)}, u32[]{:S(2)}, u32[]{:S(2)}) collective-permute-start(bf16[256,768]{1,0:T(8,128)(2,1)S(1)} %bitcast.613), channel_id=1, source_target_pairs={{0,4},{4,0},{8,12},{12,8},{1,5},{5,1},{9,13},{13,9},{2,6},{6,2},{1... | collective-permute-start | bytes 1179656 | tf_op jit(solution)/shard_map/ppermute | solution.py:126
  48.8 15.4 %collective-permute-start.8 = (bf16[256,896]{1,0:T(8,128)(2,1)S(1)}, bf16[256,896]{1,0:T(8,128)(2,1)S(1)}, u32[]{:S(2)}, u32[]{:S(2)}) collective-permute-start(bf16[256,896]{1,0:T(8,128)(2,1)S(1)} %bitcast.609), channel_id=1, source_target_pairs={{0,32},{32,0},{64,96},{96,64},{1,33},{33,1},{65,97},{97,65},{2,34}... | collective-permute-start | bytes 1376264 | tf_op jit(solution)/shard_map/ppermute | solution.py:126
  57.8 12.6 %collective-permute-start.23 = (bf16[128,2304]{1,0:T(8,128)(2,1)S(1)}, bf16[128,2304]{1,0:T(8,128)(2,1)S(1)}, u32[]{:S(2)}, u32[]{:S(2)}) collective-permute-start(bf16[128,2304]{1,0:T(8,128)(2,1)S(1)} %bitcast.598), channel_id=1, source_target_pairs={{0,4},{4,0},{8,12},{12,8},{1,5},{5,1},{9,13},{13,9},{2,6},{6,2},{1... | collective-permute-start | bytes 1769480 | tf_op jit(solution)/shard_map/ppermute | solution.py:126
  64.4 22.6 %collective-permute-start.11 = (bf16[512,768]{1,0:T(8,128)(2,1)S(1)}, bf16[512,768]{1,0:T(8,128)(2,1)S(1)}, u32[]{:S(2)}, u32[]{:S(2)}) collective-permute-start(bf16[512,768]{1,0:T(8,128)(2,1)S(1)} %bitcast.587), channel_id=1, source_target_pairs={{0,2},{2,0},{1,3},{3,1},{4,6},{6,4},{5,7},{7,5},{8,10},{10,8},{9,1... | collective-permute-start | bytes 2359304 | tf_op jit(solution)/shard_map/ppermute | solution.py:126
  64.5 21.3 %collective-permute-start.10 = (bf16[512,896]{1,0:T(8,128)(2,1)S(1)}, bf16[512,896]{1,0:T(8,128)(2,1)S(1)}, u32[]{:S(2)}, u32[]{:S(2)}) collective-permute-start(bf16[512,896]{1,0:T(8,128)(2,1)S(1)} %bitcast.557), channel_id=1, source_target_pairs={{0,2},{2,0},{1,3},{3,1},{4,6},{6,4},{5,7},{7,5},{8,10},{10,8},{9,1... | collective-permute-start | bytes 2752520 | tf_op jit(solution)/shard_map/ppermute | solution.py:126
  73.2 26.5 %collective-permute-start.27 = (bf16[256,2304]{1,0:T(8,128)(2,1)}, bf16[256,2304]{1,0:T(8,128)(2,1)}, u32[]{:S(2)}, u32[]{:S(2)}) collective-permute-start(bf16[256,2304]{1,0:T(8,128)(2,1)} %bitcast.97), channel_id=1, source_target_pairs={{0,96},{32,64},{64,32},{96,0},{1,97},{33,65},{65,33},{97,1},{2,98}... | collective-permute-start | bytes 3538952 | tf_op jit(solution)/shard_map/ppermute | solution.py:126
  75.4 26.2 %collective-permute-start.26 = (bf16[256,2304]{1,0:T(8,128)(2,1)}, bf16[256,2304]{1,0:T(8,128)(2,1)}, u32[]{:S(2)}, u32[]{:S(2)}) collective-permute-start(bf16[256,2304]{1,0:T(8,128)(2,1)} %bitcast.93), channel_id=1, source_target_pairs={{0,12},{4,8},{8,4},{12,0},{1,13},{5,9},{9,5},{13,1},{2,14},{6,10},... | collective-permute-start | bytes 3538952 | tf_op jit(solution)/shard_map/ppermute | solution.py:126
  75.4 33.7 %collective-permute-start.25 = (bf16[256,2304]{1,0:T(8,128)(2,1)}, bf16[256,2304]{1,0:T(8,128)(2,1)}, u32[]{:S(2)}, u32[]{:S(2)}) collective-permute-start(bf16[256,2304]{1,0:T(8,128)(2,1)} %bitcast.89), channel_id=1, source_target_pairs={{0,32},{32,0},{64,96},{96,64},{1,33},{33,1},{65,97},{97,65},{2,34}... | collective-permute-start | bytes 3538952 | tf_op jit(solution)/shard_map/ppermute | solution.py:126
  110.8 12.2 %collective-permute-start.28 = (bf16[512,2304]{1,0:T(8,128)(2,1)S(1)}, bf16[512,2304]{1,0:T(8,128)(2,1)S(1)}, u32[]{:S(2)}, u32[]{:S(2)}) collective-permute-start(bf16[512,2304]{1,0:T(8,128)(2,1)S(1)} %bitcast.544), channel_id=1, source_target_pairs={{0,2},{2,0},{1,3},{3,1},{4,6},{6,4},{5,7},{7,5},{8,10},{10,8},{9,1... | collective-permute-start | bytes 7077896 | tf_op jit(solution)/shard_map/ppermute | solution.py:126
  111.7 12.7 %collective-permute-start.30 = (bf16[512,2304]{1,0:T(8,128)(2,1)S(1)}, bf16[512,2304]{1,0:T(8,128)(2,1)S(1)}, u32[]{:S(2)}, u32[]{:S(2)}) collective-permute-start(bf16[512,2304]{1,0:T(8,128)(2,1)S(1)} %bitcast.550), channel_id=1, source_target_pairs={{0,2},{2,0},{1,3},{3,1},{4,6},{6,4},{5,7},{7,5},{8,10},{10,8},{9,1... | collective-permute-start | bytes 7077896 | tf_op jit(solution)/shard_map/ppermute | solution.py:126
  131.7 13.0 %collective-permute-start.34 = (bf16[512,2304]{1,0:T(8,128)(2,1)S(1)}, bf16[512,2304]{1,0:T(8,128)(2,1)S(1)}, u32[]{:S(2)}, u32[]{:S(2)}) collective-permute-start(bf16[512,2304]{1,0:T(8,128)(2,1)S(1)} %convolution_convert_fusion), channel_id=1, source_target_pairs={{0,2},{2,0},{1,3},{3,1},{4,6},{6,4},{5,7},{7,5},{8,10},{10,8},{9,1... | collective-permute-start | bytes 7077896 | tf_op jit(solution)/shard_map/ppermute | solution.py:126
  132.8 14.1 %collective-permute-start.35 = (bf16[128,1024]{0,1:T(8,128)(2,1)S(1)}, bf16[128,1024]{0,1:T(8,128)(2,1)S(1)}, u32[]{:S(2)}, u32[]{:S(2)}) collective-permute-start(bf16[128,1024]{0,1:T(8,128)(2,1)S(1)} %pad_maximum_fusion.22), channel_id=1, source_target_pairs={{0,1},{1,0},{2,3},{3,2},{4,5},{5,4},{6,7},{7,6},{8,9},{9,8},{10,11... | collective-permute-start | bytes 786440 | tf_op jit(solution)/shard_map/ppermute | solution.py:130
  155.4 19.7 %collective-permute-start.37 = (bf16[256,1536]{1,0:T(8,128)(2,1)S(1)}, bf16[256,1536]{1,0:T(8,128)(2,1)S(1)}, u32[]{:S(2)}, u32[]{:S(2)}) collective-permute-start(bf16[256,1536]{1,0:T(8,128)(2,1)S(1)} %bitcast.592), channel_id=1, source_target_pairs={{0,32},{32,0},{64,96},{96,64},{1,33},{33,1},{65,97},{97,65},{2,34}... | collective-permute-start | bytes 2359304 | tf_op jit(solution)/shard_map/ppermute | solution.py:126
  155.8 20.6 %collective-permute-start.36 = (bf16[256,1536]{1,0:T(8,128)(2,1)S(1)}, bf16[256,1536]{1,0:T(8,128)(2,1)S(1)}, u32[]{:S(2)}, u32[]{:S(2)}) collective-permute-start(bf16[256,1536]{1,0:T(8,128)(2,1)S(1)} %bitcast.591), channel_id=1, source_target_pairs={{0,12},{4,8},{8,4},{12,0},{1,13},{5,9},{9,5},{13,1},{2,14},{6,10},... | collective-permute-start | bytes 2359304 | tf_op jit(solution)/shard_map/ppermute | solution.py:126
  159.4 20.4 %collective-permute-start.38 = (bf16[256,1536]{1,0:T(8,128)(2,1)S(1)}, bf16[256,1536]{1,0:T(8,128)(2,1)S(1)}, u32[]{:S(2)}, u32[]{:S(2)}) collective-permute-start(bf16[256,1536]{1,0:T(8,128)(2,1)S(1)} %bitcast.590), channel_id=1, source_target_pairs={{0,96},{32,64},{64,32},{96,0},{1,97},{33,65},{65,33},{97,1},{2,98}... | collective-permute-start | bytes 2359304 | tf_op jit(solution)/shard_map/ppermute | solution.py:126
  162.5 27.2 %collective-permute-start.39 = (bf16[256,2304]{1,0:T(8,128)(2,1)S(1)}, bf16[256,2304]{1,0:T(8,128)(2,1)S(1)}, u32[]{:S(2)}, u32[]{:S(2)}) collective-permute-start(bf16[256,2304]{1,0:T(8,128)(2,1)S(1)} %bitcast.580), channel_id=1, source_target_pairs={{0,4},{4,0},{8,12},{12,8},{1,5},{5,1},{9,13},{13,9},{2,6},{6,2},{1... | collective-permute-start | bytes 3538952 | tf_op jit(solution)/shard_map/ppermute | solution.py:126
  194.3 14.6 %collective-permute-start.43 = (bf16[128,2304]{1,0:T(8,128)(2,1)S(1)}, bf16[128,2304]{1,0:T(8,128)(2,1)S(1)}, u32[]{:S(2)}, u32[]{:S(2)}) collective-permute-start(bf16[128,2304]{1,0:T(8,128)(2,1)S(1)} %bitcast.603), channel_id=1, source_target_pairs={{0,12},{4,8},{8,4},{12,0},{1,13},{5,9},{9,5},{13,1},{2,14},{6,10},... | collective-permute-start | bytes 1769480 | tf_op jit(solution)/shard_map/ppermute | solution.py:126
  212.3 17.2 %collective-permute-start.51 = (bf16[128,1024]{0,1:T(8,128)(2,1)}, bf16[128,1024]{0,1:T(8,128)(2,1)}, u32[]{:S(2)}, u32[]{:S(2)}) collective-permute-start(bf16[128,1024]{0,1:T(8,128)(2,1)} %get-tuple-element.191), channel_id=1, source_target_pairs={{0,1},{1,0},{2,3},{3,2},{4,5},{5,4},{6,7},{7,6},{8,9},{9,8},{10,11... | collective-permute-start | bytes 786440 | tf_op jit(solution)/shard_map/ppermute | solution.py:130
  213.0 16.6 %collective-permute-start.52 = (bf16[128,1024]{0,1:T(8,128)(2,1)}, bf16[128,1024]{0,1:T(8,128)(2,1)}, u32[]{:S(2)}, u32[]{:S(2)}) collective-permute-start(bf16[128,1024]{0,1:T(8,128)(2,1)} %pad_maximum_fusion.23), channel_id=1, source_target_pairs={{0,1},{1,0},{2,3},{3,2},{4,5},{5,4},{6,7},{7,6},{8,9},{9,8},{10,11... | collective-permute-start | bytes 786440 | tf_op jit(solution)/shard_map/ppermute | solution.py:130
  256.9 12.8 %collective-permute-start.74 = (bf16[16,1536]{1,0:T(8,128)(2,1)S(1)}, bf16[16,1536]{1,0:T(8,128)(2,1)S(1)}, u32[]{:S(2)}, u32[]{:S(2)}) collective-permute-start(bf16[16,1536]{1,0:T(8,128)(2,1)S(1)} %slice_bitcast_fusion.41), channel_id=1, source_target_pairs={{0,16},{16,0},{1,17},{17,1},{2,18},{18,2},{3,19},{19,3},{4,20},{20... | collective-permute-start | bytes 147464 | tf_op jit(solution)/shard_map/ppermute | solution.py:126
  257.8 26.9 %collective-permute-start.75 = (bf16[16,2304]{1,0:T(8,128)(2,1)S(1)}, bf16[16,2304]{1,0:T(8,128)(2,1)S(1)}, u32[]{:S(2)}, u32[]{:S(2)}) collective-permute-start(bf16[16,2304]{1,0:T(8,128)(2,1)S(1)} %slice_bitcast_fusion.33), channel_id=1, source_target_pairs={{0,16},{16,0},{1,17},{17,1},{2,18},{18,2},{3,19},{19,3},{4,20},{20... | collective-permute-start | bytes 221192 | tf_op jit(solution)/shard_map/ppermute | solution.py:126
  (124 other events, 1016.3 us)
